TPU v7x, 512 devices: a whole 4x8x8 slice. The times are simulated.
512 devices in a mesh: dp: 16 (over y_hi, x), fsdp: 32 (over z, y_lo, core).
Axes of the slice: x: 4, y: 8 (y_hi: 4, y_lo: 2; y = y_hi * 2 + y_lo), z: 8, core: 2. Of those that a mesh axis runs over, the one named last changes fastest.
Arguments:
- tokens: bfloat16 [65536, 8192], P(('dp', 'fsdp')), may hold values from -6 to 6
- frozen_key_matrix: bfloat16 [8192, 512], P('fsdp'), may hold values from -0.0625 to 0.0625
- adapter_down_factor: float32 [96, 8192, 16], P('fsdp', 'dp'), may hold values from -0.0625 to 0.0625
- adapter_up_factor: float32 [96, 16, 512], P('fsdp', None, 'dp'), may hold values from -1.5 to 1.5
- key_norm_gain: float32 [128], replicated, may hold values from 0.1 to 1.9
- adapter_offset: int32 [16, 32], P('dp', 'fsdp'), may hold values from 0 to 2, as said below
- loss_row_count: int32 [16, 32], P('dp', 'fsdp'), may hold values from 32 to 128, as said below
- cotangent: bfloat16 [65536, 512], P(('dp', 'fsdp')), may hold values from -6 to 6
Outputs:
- keys: bfloat16 [65536, 512], P(('dp', 'fsdp'))
- input_grad: bfloat16 [65536, 8192], P(('dp', 'fsdp'))
- down_grad: float32 [96, 8192, 16], P('fsdp', 'dp')
- up_factor_gradient: float32 [96, 16, 512], P('fsdp', None, 'dp')
Inputs may be any that keep to these rules, and one draw needn't show every extreme that they name: `adapter_offset`: in every column j, each offset 0 to 2 is named by at least one dp index. `loss_row_count`: some block has 128 live rows and some block 32.
All inputs are finite; a program needn't handle non-finite values.
Results may differ from a plain program's by a relative error of at most 0.0033.
Values may be sent and summed in bfloat16 or wider, within the bound.
A program may use at most 64 MiB of HBM per device.

v0:
```python
import jax
import jax.numpy as jnp
from jax import lax
from jax.sharding import PartitionSpec as P

HD = 128


adapter_scale = 2.0
norm_eps = 1e-06


def on_device(
    tokens,
    frozen_key_matrix,
    adapter_down_factor,
    adapter_up_factor,
    key_norm_gain,
    adapter_offset,
    loss_row_count,
    cotangent,
):
    highest_precision = lax.Precision.HIGHEST
    row_count = tokens.shape[0]
    key_width = frozen_key_matrix.shape[1]
    stored_values = adapter_down_factor.shape[0]
    slot_value = adapter_offset[0, 0]
    live_count = loss_row_count[0, 0]
    selector = jnp.arange(stored_values, dtype=jnp.int32) == slot_value
    counted = jnp.where(selector, live_count, 0)
    summed_rows = lax.psum(counted, "dp")
    adapter_total = jnp.sum(jnp.where(selector, summed_rows, 0)).astype(jnp.float32)
    down_whole, up_whole = (
        lax.all_gather(adapter_down_factor, "dp", axis=1, tiled=True),
        lax.all_gather(adapter_up_factor, "dp", axis=2, tiled=True),
    )
    down_projection = lax.dynamic_index_in_dim(down_whole, slot_value, 0, keepdims=False)
    up_projection = lax.dynamic_index_in_dim(up_whole, slot_value, 0, keepdims=False)
    weight = lax.all_gather(frozen_key_matrix, "fsdp", axis=0, tiled=True)
    frozen_output = jnp.dot(tokens, weight, preferred_element_type=jnp.float32)
    tokens_float = tokens.astype(jnp.float32)
    lowrank_output = jnp.dot(tokens_float, down_projection, precision=highest_precision)
    projected_keys = frozen_output + adapter_scale * jnp.dot(
        lowrank_output, up_projection, precision=highest_precision
    )
    shaped = projected_keys.reshape(row_count, -1, HD)
    mean_square = jnp.mean(shaped * shaped, axis=-1, keepdims=True)
    inverse_rms = lax.rsqrt(mean_square + norm_eps)
    normed = shaped * inverse_rms
    keys = (normed * key_norm_gain).reshape(row_count, key_width).astype(jnp.bfloat16)
    row_mask = (jnp.arange(row_count, dtype=jnp.int32) < live_count).astype(jnp.float32)
    row_grad = cotangent.astype(jnp.float32) * row_mask[:, None] * (row_count / adapter_total)
    scaled_grad = row_grad.reshape(normed.shape) * key_norm_gain
    along_norm = jnp.mean(scaled_grad * normed, axis=-1, keepdims=True)
    prenorm_gradient = (inverse_rms * (scaled_grad - normed * along_norm)).reshape(
        row_count, key_width
    )
    pre_grad_low = prenorm_gradient.astype(jnp.bfloat16)
    lowrank_gradient = adapter_scale * jnp.dot(
        prenorm_gradient, up_projection.T, precision=highest_precision
    )
    input_base = lax.dot_general(
        pre_grad_low, weight, (((1,), (1,)), ((), ())), preferred_element_type=jnp.float32
    )
    input_grad = (
        input_base + jnp.dot(lowrank_gradient, down_projection.T, precision=highest_precision)
    ).astype(jnp.bfloat16)
    down_grad = lax.dot_general(
        tokens_float, lowrank_gradient, (((0,), (0,)), ((), ())), precision=highest_precision
    )
    up_factor_gradient = adapter_scale * lax.dot_general(
        lowrank_output, prenorm_gradient, (((0,), (0,)), ((), ())), precision=highest_precision
    )
    selector_float = selector.astype(jnp.float32)
    down_terms = selector_float[:, None, None] * down_grad[None]
    up_terms = selector_float[:, None, None] * up_factor_gradient[None]
    down_sum, up_sum = (
        lax.psum_scatter(down_terms, "dp", scatter_dimension=1, tiled=True),
        lax.psum_scatter(up_terms, "dp", scatter_dimension=2, tiled=True),
    )
    return (keys, input_grad, down_sum, up_sum)


def solution(mesh):
    placed = (
        P(("dp", "fsdp"), None),
        P("fsdp", None),
        P("fsdp", "dp", None),
        P("fsdp", None, "dp"),
        P(),
        P("dp", "fsdp"),
        P("dp", "fsdp"),
        P(("dp", "fsdp"), None),
    )
    return jax.shard_map(
        on_device,
        mesh=mesh,
        in_specs=placed,
        out_specs=(
            P(("dp", "fsdp"), None),
            P(("dp", "fsdp"), None),
            P("fsdp", "dp", None),
            P("fsdp", None, "dp"),
        ),
        check_vma=False,
    )
```

profile of v0, /device:TPU:1, one launch (start us, length us, event | category | flops | bytes accessed | tf_op | source)
XLA Modules:
  0.0 359.8 jit_solution(965696795780993262)
XLA Ops:
  7.2 0.0 copy-start
  7.2 0.0 copy-start.2
  7.2 0.0 all-gather.5.cloned.1.call-start
  7.2 0.7 all-gather.5.cloned.1.call-update
  7.9 0.0 all-gather.3.cloned.1.call-start
  8.0 0.7 all-gather.3.cloned.1.call-update
  8.7 0.0 reduce-scatter.7.cloned.1.call-start
  10.0 16.1 %psum.7 = s32[3]{0:T(128)S(1)} all-reduce(s32[3]{0:T(128)S(1)} %fusion.12), channel_id=1, replica_groups=mesh['dp'=16,'fsdp'=32] {'dp'}, use_global_device_ids=true, to_apply=%region_1.2 | all-reduce | flops 3 | bytes 24 | tf_op jit(solution)/shard_map/psum | solution.py:31
  26.1 0.8 copy.12
  26.9 0.6 select_reduce_fusion
  28.3 1.0 multiply_multiply_fusion
  29.3 0.1 reshape.48
  29.4 51.7 %all_gather.11 = f32[3,16,512]{1,0,2:T(4,128)S(1)} all-gather(f32[3,16,32]{1,0,2:T(4,128)S(1)} %copy.12), channel_id=1, replica_groups=mesh['dp'=16,'fsdp'=32] {'dp'}, dimensions={2}, use_global_device_ids=true | all-gather | bytes 104448 | tf_op jit(solution)/shard_map/all_gather | solution.py:35
  81.1 0.2 constant_dynamic-slice_fusion
  81.3 0.0 copy-done.2
  81.3 1.4 all-gather.5.cloned.1.call-done
  82.7 0.0 copy-done
  82.7 2.8 fusion.3
  85.5 73.2 %all-gather.3.cloned.1.call-done = bf16[8192,512]{1,0:T(8,128)(2,1)} async-done(((bf16[256,512]{1,0:T(8,128)(2,1)}), bf16[8192,512]{1,0:T(8,128)(2,1)}) %all-gather.3.cloned.1.call-update) | async-done | bytes 8388624 | tf_op jit(solution)/shard_map/all_gather | solution.py:39
  158.6 4.6 %fusion.15 = f32[128,512]{1,0:T(8,128)S(1)} fusion(bf16[128,8192]{1,0:T(8,128)(2,1)S(1)} %copy-done, bf16[8192,512]{1,0:T(8,128)(2,1)} %all-gather.3.cloned.1.call-done), kind=kOutput, calls=%fused_computation.35 | convolution fusion | flops 1073741824 | bytes 10747904 | tf_op jit(solution)/shard_map/dot_general | solution.py:40
  163.3 0.0 copy-start.1
  163.3 0.4 fusion.1
  163.7 0.1 reshape.47
  163.8 0.2 multiply_reduce_fusion.1
  164.1 0.4 multiply_reduce_fusion
  164.5 0.2 mul.139
  164.7 0.2 mul.123
  164.9 0.0 copy-done.1
  164.9 0.7 fusion.8
  165.6 0.5 convolution_multiply_fusion.2
  166.1 0.3 convolution_multiply_fusion.1
  166.4 1.7 convolution_bitcast_fusion
  168.1 0.1 broadcast_multiply_fusion.1
  168.2 0.4 copy.13
  168.6 1.1 reshape.49
  169.7 0.0 reduce-scatter.7.cloned.1.call-update
  169.7 0.0 reduce-scatter.5.cloned.1.call-start
  169.7 2.4 broadcast_multiply_fusion
  172.1 0.0 reduce-scatter.5.cloned.1.call-update
  172.1 6.2 %fusion.9 = f32[128,8192]{1,0:T(8,128)S(1)} fusion(bf16[8192,512]{1,0:T(8,128)(2,1)} %all-gather.3.cloned.1.call-done, f32[128,512]{1,0:T(8,128)S(1)} %get-tuple-element.4), kind=kOutput, calls=%fused_computation.21 | convolution fusion | flops 1073807360 | bytes 12845056 | tf_op jit(solution)/shard_map/dot_general | solution.py:62
  178.3 5.9 %fusion = bf16[128,8192]{1,0:T(8,128)(2,1)} fusion(f32[128,8192]{1,0:T(8,128)S(1)} %fusion.9, f32[128,16]{0,1:T(8,128)S(1)} %convolution_multiply_fusion.2, f32[3,8192,16]{1,2,0:T(8,128)} %all-gather.5.cloned.1.call-done, s32[]{:T(128)S(6)} %select_n.14), kind=kOutput, calls=%fused_computation.1 | convolution fusion | flops 203423744 | bytes 6823940 | tf_op jit(solution)/shard_map/dot_general | solution.py:66
  184.2 73.5 %reduce-scatter.7.cloned.1.call-done = f32[32,48]{1,0:T(8,128)} async-done(((f32[512,48]{1,0:T(8,128)}), f32[32,48]{1,0:T(8,128)}) %reduce-scatter.7.cloned.1.call-update) | async-done | bytes 6160
  257.7 0.8 reshape.50
  258.6 0.7 copy.14
  259.2 94.1 %reduce-scatter.5.cloned.1.call-done = f32[3,512,16]{1,2,0:T(8,128)} async-done(((f32[3,8192,16]{1,2,0:T(8,128)}), f32[3,512,16]{1,2,0:T(8,128)}) %reduce-scatter.5.cloned.1.call-update) | async-done | bytes 98320 | tf_op jit(solution)/shard_map/reduce_scatter | solution.py:78
  (6 shorter events, 0.0 us)
Async XLA Ops:
  7.2 75.5 %copy-start = (bf16[128,8192]{1,0:T(8,128)(2,1)S(1)}, bf16[128,8192]{1,0:T(8,128)(2,1)}, u32[]{:S(2)}) copy-start(bf16[128,8192]{1,0:T(8,128)(2,1)} %param.8) | copy-start | bytes 6291460
  7.2 74.1 %copy-start.2 = (f32[128]{0:T(128)S(1)}, f32[128]{0:T(128)}, u32[]{:S(2)}) copy-start(f32[128]{0:T(128)} %param.12) | copy-start | bytes 1540
  7.2 75.5 %all-gather.5.cloned.1.call-start = ((), (), s32[]{:S(2)}) async-start(), calls=%async_computation.3 | async-start | bytes 1671168 | tf_op jit(solution)/shard_map/all_gather | solution.py:34
  7.9 150.7 %all-gather.3.cloned.1.call-start = ((), (), s32[]{:S(2)}) async-start(), calls=%async_computation.2 | async-start | bytes 8650752 | tf_op jit(solution)/shard_map/all_gather | solution.py:39
  8.7 249.1 %reduce-scatter.7.cloned.1.call-start = ((), (), s32[]{:S(2)}) async-start(), calls=%async_computation.5 | async-start | bytes 278528
  163.3 1.6 copy-start.1
  169.7 183.6 %reduce-scatter.5.cloned.1.call-start = ((), (), s32[]{:S(2)}) async-start(), calls=%async_computation.4 | async-start | bytes 1671168 | tf_op jit(solution)/shard_map/reduce_scatter | solution.py:78
Sparse Core Ops, SparseCore 0:
  11.0 71.5 all-gather.4
  84.8 73.7 all-gather.2
  169.8 87.8 reduce-scatter.6
  262.8 90.4 reduce-scatter.4
where the time goes:
time: 361 us; the launch traced here: 360 us
  waiting for transfers between devices  244 us (68%)
  blocking collectives  67.8 us (19%)
  matrix products  22.4 us (6%)
  between operations  15.9 us (4%)
  other arithmetic  5.37 us (1%)
  local copies, waits for them, and re-layouts  4.64 us (1%)
    reduce_scatter x1, waiting for transfers between devices, on_device(): lax.psum_scatter(down_terms, 'dp', scatter_dimension=1, tiled=True)  94.1 us
    unnamed x5, waiting for transfers between devices  74.9 us
    all_gather x1, waiting for transfers between devices, on_device(): weight = lax.all_gather(frozen_key_matrix, 'fsdp', axis=0, tiled=True)  73.2 us
    all_gather x1, blocking collectives, on_device(): lax.all_gather(adapter_up_factor, 'dp', axis=2, tiled=True)  51.7 us
    psum x1, blocking collectives, on_device(): summed_rows = lax.psum(counted, 'dp')  16.1 us
  transfers between devices with their start and end apart: 4, of which 4 were waited for; matrix products, arithmetic and copies ran while one was open for 6% of the time, Pallas kernels for 0%

commit v1 on v0

v1 whole, which is shorter than its diff:
```python
import functools

import jax
import jax.numpy as jnp
from jax import lax
from jax.experimental import pallas as pl
from jax.experimental.pallas import tpu as pltpu
from jax.sharding import PartitionSpec as P

HD = 128
SCALE = 2.0
EPS = 1e-06
NX, NYH, NZ = 4, 4, 8
NDP = NX * NYH
NFS = NZ * 4
RANK = 16
SLOTS = 3
BF, F32, I32 = jnp.bfloat16, jnp.float32, jnp.int32
HIGH = lax.Precision.HIGHEST
MINOR = (((1,), (1,)), ((), ()))
PLAIN = (((1,), (0,)), ((), ()))
EXCL = 96
FETCH = 256 - EXCL
HALF = FETCH // 2
XHALF = EXCL // 2


def dot(a, b, dims, precision=None):
    return lax.dot_general(a, b, dims, precision=precision, preferred_element_type=F32)


def split(v):
    hi = v.astype(BF)
    return hi, (v - hi.astype(F32)).astype(BF)


def kernel(
    off_ref, cnt_ref, gain_ref, down_ref, up_ref, cot_ref, tok_hbm, w_hbm,
    keys_ref, down_out, up_out, ig_hbm,
    wf, tok, ig, acc, pg, meta, msg_out, msg_in, gmsg_out, gmsg_in, upf, ups,
    loc_sem, ig_sem, zs, zr, ys, yr, xs, xr, ds_, dr, ms, mr, fs, fr, gs, gr,
):
    i, j = lax.axis_index("dp"), lax.axis_index("fsdp")
    yh, x = i // NX, i % NX
    z, yl, c = j // 4, (j // 2) % 2, j % 2
    px = x % 2

    def dp_of(a, b):
        return a * NX + b

    z_up = (i, (j + 4) % NFS)
    z_dn = (i, (j + NFS - 4) % NFS)
    sib = (i, j + 1 - 2 * c)
    jy = j + 2 - 4 * yl
    y_up = (dp_of((yh + yl) % NYH, x), jy)
    y_dn = (dp_of((yh + NYH - 1 + yl) % NYH, x), jy)
    x_up = (dp_of(yh, (x + 1) % NX), j)
    x_dn = (dp_of(yh, (x + NX - 1) % NX), j)

    def peer(r):
        return (i + r) % NDP

    tok_copy = pltpu.make_async_copy(tok_hbm, tok, loc_sem.at[0])
    tok_copy.start()
    pair_me = j // 2
    own = pltpu.make_async_copy(w_hbm, wf.at[pair_me, pl.ds(pl.multiple_of(256 * c, 256), 256)], loc_sem.at[1])
    own.start()

    off, cnt = off_ref[0, 0], cnt_ref[0, 0]
    rows8 = lax.broadcasted_iota(I32, (8, 128), 0)
    meta[i] = jnp.where(rows8 < 4, jnp.full((8, 128), off, I32), jnp.full((8, 128), cnt, I32))

    barrier = pltpu.get_barrier_semaphore()

    def greet(d):
        pl.semaphore_signal(barrier, inc=1, device_id=d, device_id_type=pl.DeviceIdType.MESH)

    for d in (z_up, z_dn, y_up, y_dn, sib):
        greet(d)

    @pl.loop(1, NDP)
    def _(r):
        greet((peer(r), j))

    pl.semaphore_wait(barrier, 5 + NDP - 1)

    def remote(src, dst, ssem, rsem, to):
        return pltpu.make_async_remote_copy(
            src_ref=src, dst_ref=dst, send_sem=ssem, recv_sem=rsem, device_id=to, device_id_type=pl.DeviceIdType.MESH
        )

    def rows(dz, par, start, size):
        zz = (z + dz + NZ) % NZ
        q = zz * 2 + (yl + par) % 2
        return wf.at[q, pl.ds(pl.multiple_of(256 * c + start, 16), size)]

    f0 = px * EXCL
    x0 = px * FETCH
    xo = (1 - px) * FETCH
    order = [(0, 0), (-1, 0), (1, 0), (0, 1), (-2, 0), (2, 0), (-1, 1), (1, 1),
             (-3, 0), (3, 0), (-2, 1), (2, 1), (4, 0), (-3, 1), (3, 1), (4, 1)]
    spot = {s: n for n, s in enumerate(order)}
    sends = []

    def send(src, ssem, rsem, to):
        copy = remote(src, src, ssem, rsem, to)
        copy.start()
        sends.append(copy)

    def arrived(ref, ssem, rsem):
        remote(ref, ref, ssem, rsem, sib).wait_recv()

    def z_piece(hop, dz):
        if hop < 4:
            return rows(dz, 0, f0, FETCH)
        return rows(dz, 0, f0 if dz < 0 else f0 + HALF, HALF)

    def send_z(hop):
        send(z_piece(hop, -(hop - 1) if hop < 4 else -3), zs.at[hop - 1], zr.at[hop - 1], z_up)
        send(z_piece(hop, hop - 1 if hop < 4 else 3), zs.at[3 + hop], zr.at[3 + hop], z_dn)

    def wait_z(hop):
        if hop < 4:
            arrived(rows(-hop, 0, f0, FETCH), zs.at[hop - 1], zr.at[hop - 1])
            arrived(rows(hop, 0, f0, FETCH), zs.at[3 + hop], zr.at[3 + hop])
        else:
            arrived(rows(4, 0, f0, HALF), zs.at[3], zr.at[3])
            arrived(rows(4, 0, f0 + HALF, HALF), zs.at[7], zr.at[7])

    def send_y(dz):
        n = 2 * (dz + 3)
        send(rows(dz, 0, f0, HALF), ys.at[n], yr.at[n], y_up)
        send(rows(dz, 0, f0 + HALF, HALF), ys.at[n + 1], yr.at[n + 1], y_dn)

    def wait_y(dz):
        n = 2 * (dz + 3)
        arrived(rows(dz, 1, f0, HALF), ys.at[n], yr.at[n])
        arrived(rows(dz, 1, f0 + HALF, HALF), ys.at[n + 1], yr.at[n + 1])

    def send_x(dz, par):
        n = 2 * spot[dz, par]
        send(rows(dz, par, x0, XHALF), xs.at[n], xr.at[n], x_up)
        send(rows(dz, par, x0 + XHALF, XHALF), xs.at[n + 1], xr.at[n + 1], x_dn)

    def wait_x(dz, par):
        n = 2 * spot[dz, par]
        arrived(rows(dz, par, xo, XHALF), xs.at[n], xr.at[n])
        arrived(rows(dz, par, xo + XHALF, XHALF), xs.at[n + 1], xr.at[n + 1])

    def send_d(dz, par):
        n = spot[dz, par]
        send(rows(dz, par, 0, 256), ds_.at[n], dr.at[n], sib)

    def wait_d(dz, par):
        n = spot[dz, par]
        zz = (z + dz + NZ) % NZ
        q = zz * 2 + (yl + par) % 2
        ref = wf.at[q, pl.ds(pl.multiple_of(256 * (1 - c), 256), 256)]
        arrived(ref, ds_.at[n], dr.at[n])
        return q

    own.wait()
    send_z(1)
    send_y(0)
    send_d(0, 0)

    @pl.loop(1, NDP)
    def _(r):
        remote(meta.at[i], meta.at[i], ms.at[r], mr.at[r], (peer(r), j)).start()

    acc[...] = jnp.zeros_like(acc)
    ups[...] = jnp.zeros_like(ups)
    ups[:, :, 0:32] = up_ref[...]
    quarter = i % 4

    def placed(v):
        out = v
        for n in range(1, 4):
            out = jnp.where(quarter == n, pltpu.roll(v, 32 * n, 1), out)
        return out

    for s in range(SLOTS):
        ups[s] = placed(ups[s])

    @pl.loop(1, NDP)
    def _(r):
        from_ = (i + NDP - r) % NDP
        remote(meta.at[from_], meta.at[from_], ms.at[r], mr.at[r], sib).wait_recv()

    def chosen(o, width, ref):
        o = jnp.broadcast_to(o[0:1, 0:1], (RANK, width))
        return jnp.where(o == 0, ref[0], jnp.where(o == 1, ref[1], ref[2]))

    def build(p, dst):
        o = meta[p]
        dst[:, 0:512] = chosen(o, 512, down_ref).astype(BF)
        hi, lo = split(chosen(o, 128, ups))
        dst[:, 512:640] = hi
        dst[:, 640:768] = lo

    build(i, msg_in.at[i])

    @pl.loop(1, NDP)
    def _(r):
        p = peer(r)
        build(p, msg_out.at[p])
        remote(msg_out.at[p], msg_in.at[i], fs.at[r], fr.at[r], (p, j)).start()

    def product(q):
        cols = pl.ds(pl.multiple_of(512 * q, 512), 512)
        acc[...] += dot(tok[:, cols], wf[q], PLAIN)

    tok_copy.wait()

    wait_z(1)
    send_z(2)
    send_y(-1)
    send_y(1)
    send_x(-1, 0)
    send_x(1, 0)
    wait_y(0)
    send_x(0, 1)
    product(wait_d(0, 0))
    wait_z(2)
    send_z(3)
    send_y(-2)
    send_y(2)
    send_x(-2, 0)
    send_x(2, 0)
    wait_x(-1, 0)
    send_d(-1, 0)
    wait_x(1, 0)
    send_d(1, 0)
    wait_y(-1)
    send_x(-1, 1)
    wait_y(1)
    send_x(1, 1)
    wait_x(0, 1)
    send_d(0, 1)
    wait_z(3)
    send_z(4)
    send_y(-3)
    send_y(3)
    send_x(-3, 0)
    send_x(3, 0)
    wait_x(-2, 0)
    send_d(-2, 0)
    wait_x(2, 0)
    send_d(2, 0)
    wait_y(-2)
    send_x(-2, 1)
    wait_y(2)
    send_x(2, 1)
    wait_x(-1, 1)
    send_d(-1, 1)
    wait_x(1, 1)
    send_d(1, 1)
    product(wait_d(-1, 0))
    product(wait_d(1, 0))
    product(wait_d(0, 1))
    wait_z(4)
    send_y(4)
    send_x(4, 0)
    wait_x(-3, 0)
    send_d(-3, 0)
    wait_x(3, 0)
    send_d(3, 0)
    wait_y(-3)
    send_x(-3, 1)
    wait_y(3)
    send_x(3, 1)
    wait_x(-2, 1)
    send_d(-2, 1)
    wait_x(2, 1)
    send_d(2, 1)

    @pl.loop(1, NDP)
    def _(r):
        from_ = (i + NDP - r) % NDP
        remote(msg_in.at[from_], msg_in.at[from_], fs.at[r], fr.at[r], sib).wait_recv()

    def low(p, total):
        cols = pl.ds(pl.multiple_of(512 * p, 512), 512)
        return total + dot(msg_in[p, :, 0:512], tok[:, cols], MINOR)

    lr_t = lax.fori_loop(0, NDP, low, jnp.zeros((RANK, 128), F32))
    for h in range(4):
        total = jnp.zeros((RANK, 128), F32)
        for q in range(4):
            total += msg_in[4 * h + q, :, 512:640].astype(F32) + msg_in[4 * h + q, :, 640:768].astype(F32)
        upf[:, 128 * h : 128 * h + 128] = total
    up = upf[...]

    wait_y(4)
    send_x(4, 1)
    wait_x(4, 0)
    send_d(4, 0)
    wait_x(-3, 1)
    send_d(-3, 1)
    wait_x(3, 1)
    send_d(3, 1)
    for s in ((-2, 0), (2, 0), (-1, 1), (1, 1)):
        product(wait_d(*s))
    for s in ((-3, 0), (3, 0), (-2, 1), (2, 1)):
        product(wait_d(*s))
    extra = SCALE * dot(lr_t.T, up, PLAIN, HIGH)
    wait_x(4, 1)
    send_d(4, 1)
    for s in ((4, 0), (-3, 1), (3, 1), (4, 1)):
        product(wait_d(*s))

    offs, cnts = meta[:, 0, :], meta[:, 4, :]
    total = jnp.sum(jnp.where(offs == off, cnts, 0), axis=0, keepdims=True).astype(F32)
    live = lax.broadcasted_iota(I32, (128, 128), 0) < cnt
    row_scale = jnp.where(live, jnp.broadcast_to(128.0 / total, (128, 128)), 0.0)
    gain = gain_ref[...]
    for h in range(4):
        cols = slice(128 * h, 128 * h + 128)
        projected = acc[:, cols] + extra[:, cols]
        inverse = lax.rsqrt(jnp.mean(projected * projected, axis=-1, keepdims=True) + EPS)
        normed = projected * inverse
        keys_ref[:, cols] = (normed * gain).astype(BF)
        scaled = cot_ref[:, cols].astype(F32) * row_scale * gain
        along = jnp.mean(scaled * normed, axis=-1, keepdims=True)
        pg[:, cols] = inverse * (scaled - normed * along)
    pre = pg[...]
    pre_low = pre.astype(BF)
    lg_t = SCALE * dot(up, pre, MINOR, HIGH)
    hi, lo = split(lg_t)
    lg_t2 = jnp.concatenate([hi, lo], axis=0)
    lg2 = jnp.concatenate([hi.astype(F32), lo.astype(F32)], axis=0).T.astype(BF)
    upg = SCALE * dot(lr_t, pre, PLAIN, HIGH)
    upf[...] = upg

    def grads(p, dst):
        cols = pl.ds(pl.multiple_of(512 * p, 512), 512)
        both = dot(lg_t2, tok[:, cols], PLAIN)
        dst[:, 0:512] = (both[0:RANK] + both[RANK:]).astype(BF)
        hi, lo = split(upf[:, pl.ds(pl.multiple_of(128 * (p // 4), 128), 128)])
        dst[:, 512:640] = hi
        dst[:, 640:768] = lo

    @pl.loop(1, NDP)
    def _(r):
        p = peer(r)
        grads(p, gmsg_out.at[p])
        remote(gmsg_out.at[p], gmsg_in.at[i], gs.at[r], gr.at[r], (p, j)).start()

    grads(i, gmsg_in.at[i])

    def ig_copy(q):
        cols = pl.ds(pl.multiple_of(512 * q, 512), 512)
        return pltpu.make_async_copy(ig.at[:, cols], ig_hbm.at[:, cols], ig_sem.at[q])

    @pl.loop(0, NFS // 2)
    def _(q):
        cols = pl.ds(pl.multiple_of(512 * q, 512), 512)
        d = msg_in[q, :, 0:512]
        part = dot(lg2, jnp.concatenate([d, d], axis=0), PLAIN)
        ig[:, cols] = (part + dot(pre_low, wf[q], MINOR)).astype(BF)
        ig_copy(q).start()

    def gather(p, sums):
        o = jnp.broadcast_to(meta[p][0:1, 0:1], (RANK, 512))
        ou = o[:, 0:128]
        d = gmsg_in[p, :, 0:512].astype(F32)
        u = gmsg_in[p, :, 512:640].astype(F32) + gmsg_in[p, :, 640:768].astype(F32)
        return tuple(
            (sd + jnp.where(o == s, d, 0.0), su + jnp.where(ou == s, u, 0.0)) for s, (sd, su) in enumerate(sums)
        )

    zero = (jnp.zeros((RANK, 512), F32), jnp.zeros((RANK, 128), F32))
    sums = gather(i, (zero,) * SLOTS)

    def later(r, sums):
        from_ = (i + NDP - r) % NDP
        remote(gmsg_in.at[from_], gmsg_in.at[from_], gs.at[r], gr.at[r], sib).wait_recv()
        return gather(from_, sums)

    sums = lax.fori_loop(1, NDP, later, sums)
    for s, (sd, su) in enumerate(sums):
        down_out[s] = sd
        mine = su
        for n in range(1, 4):
            mine = jnp.where(quarter == n, pltpu.roll(su, 128 - 32 * n, 1), mine)
        up_out[s] = mine[:, 0:32]

    for copy in sends:
        copy.wait_send()

    @pl.loop(1, NDP)
    def _(r):
        p = peer(r)
        remote(meta.at[i], meta.at[i], ms.at[r], mr.at[r], (p, j)).wait_send()
        remote(msg_out.at[p], msg_in.at[i], fs.at[r], fr.at[r], (p, j)).wait_send()
        remote(gmsg_out.at[p], gmsg_in.at[i], gs.at[r], gr.at[r], (p, j)).wait_send()

    @pl.loop(0, NFS // 2)
    def _(q):
        ig_copy(q).wait()


def on_device(tokens, weight, down, up, gain, offset, count, cot):
    n_rows, width = tokens.shape
    keys = cot.shape[1]
    vmem = pl.BlockSpec(memory_space=pltpu.VMEM)
    smem = pl.BlockSpec(memory_space=pltpu.SMEM)
    anywhere = pl.BlockSpec(memory_space=pl.ANY)
    dma = pltpu.SemaphoreType.DMA
    down_t = jnp.transpose(down, (0, 2, 1))
    out = pl.pallas_call(
        kernel,
        out_shape=(
            jax.ShapeDtypeStruct((n_rows, keys), BF),
            jax.ShapeDtypeStruct(down_t.shape, F32),
            jax.ShapeDtypeStruct(up.shape, F32),
            jax.ShapeDtypeStruct((n_rows, width), BF),
        ),
        in_specs=[smem, smem, vmem, vmem, vmem, vmem, anywhere, anywhere],
        out_specs=(vmem, vmem, vmem, anywhere),
        scratch_shapes=[
            pltpu.VMEM((NFS // 2, 512, keys), BF),
            pltpu.VMEM((n_rows, width), BF),
            pltpu.VMEM((n_rows, width), BF),
            pltpu.VMEM((n_rows, keys), F32),
            pltpu.VMEM((n_rows, keys), F32),
            pltpu.VMEM((NDP, 8, 128), I32),
            pltpu.VMEM((NDP, RANK, 768), BF),
            pltpu.VMEM((NDP, RANK, 768), BF),
            pltpu.VMEM((NDP, RANK, 768), BF),
            pltpu.VMEM((NDP, RANK, 768), BF),
            pltpu.VMEM((RANK, keys), F32),
            pltpu.VMEM((SLOTS, RANK, 128), F32),
            dma((2,)), dma((16,)),
            dma((8,)), dma((8,)),
            dma((16,)), dma((16,)),
            dma((32,)), dma((32,)),
            dma((16,)), dma((16,)),
            dma((16,)), dma((16,)),
            dma((16,)), dma((16,)),
            dma((16,)), dma((16,)),
        ],
        compiler_params=pltpu.CompilerParams(
            collective_id=0, has_side_effects=True, vmem_limit_bytes=40 * 1024 * 1024
        ),
        name="key_projection",
    )(offset, count, gain.reshape(1, HD), down_t, up, cot, tokens, weight)
    keys_out, down_grad, up_grad, input_grad = out
    return keys_out, input_grad, jnp.transpose(down_grad, (0, 2, 1)), up_grad


def solution(mesh):
    rows = P(("dp", "fsdp"), None)
    down, up, cell = P("fsdp", "dp", None), P("fsdp", None, "dp"), P("dp", "fsdp")
    return jax.shard_map(
        on_device,
        mesh=mesh,
        in_specs=(rows, P("fsdp", None), down, up, P(), cell, cell, rows),
        out_specs=(rows, rows, down, up),
        check_vma=False,
    )
```

time: 361 us -> 77.8 us (0.22)
  waiting for transfers between devices: 244 us -> 0 us
  blocking collectives: 67.8 us -> 0 us
  Pallas kernels: 0 us -> 66.6 us
  matrix products: 22.4 us -> 0 us
  between operations: 15.9 us -> 1.95 us
  other arithmetic: 5.37 us -> 0 us
  local copies, waits for them, and re-layouts: 4.64 us -> 8.94 us
    reduce_scatter x1 -> x0, waiting for transfers between devices: 94.1 us -> none  [on_device(): lax.psum_scatter(down_terms, 'dp', scatter_dimension=1, tiled=True)]
    unnamed x5 -> x0, waiting for transfers between devices: 74.9 us -> none
    all_gather x2 -> x0, waiting for transfers between devices: 74.6 us -> none  [the longest x1 73.2 us: on_device(): weight = lax.all_gather(frozen_key_matrix, 'fsdp', axis=0, tiled=True)]
    pallas_call x0 -> x1, Pallas kernels: none -> 66.6 us  [on_device(): pl.pallas_call(kernel, out_shape=(jax.ShapeDtypeStruct((n_rows, keys), BF...]
    all_gather x1 -> x0, blocking collectives: 51.7 us -> none  [on_device(): lax.all_gather(adapter_up_factor, 'dp', axis=2, tiled=True)]
    dot_general x8 -> x0, matrix products: 22.4 us -> none  [the longest x1 6.19 us: on_device(): lax.dot_general(pre_grad_low, weight, (((1,), (1,)), ((), ())), preferred...]
    psum x1 -> x0, blocking collectives: 16.1 us -> none  [on_device(): summed_rows = lax.psum(counted, 'dp')]
    unnamed x11 -> x16, local copies, waits for them, and re-layouts: 3.83 us -> 8.94 us
  transfers between devices with their start and end apart: 4 -> 0, of which waited for: 4 -> 0; matrix products, arithmetic and copies ran while one was open for 6% -> 0% of each run, Pallas kernels for 0% -> 0%
where the time goes in v1:
time: 77.8 us; the launch traced here: 77.5 us
  Pallas kernels  66.6 us (86%)
  local copies, waits for them, and re-layouts  8.94 us (11%)
  between operations  1.95 us (3%)
    pallas_call x1, Pallas kernels, on_device(): pl.pallas_call(kernel, out_shape=(jax.ShapeDtypeStruct((n_rows, keys), BF...  66.6 us
    unnamed x16, local copies, waits for them, and re-layouts  8.94 us

profile of v1, /device:TPU:1, one launch (start us, length us, event | category | flops | bytes accessed | tf_op | source)
XLA Modules:
  0.0 77.5 jit_solution(2588943133021271201)
XLA Ops:
  1.9 0.0 copy-start
  1.9 1.6 %copy-done = bf16[128,8192]{1,0:T(8,128)(2,1)S(1)} copy-done((bf16[128,8192]{1,0:T(8,128)(2,1)S(1)}, bf16[128,8192]{1,0:T(8,128)(2,1)}, u32[]{:S(2)}) %copy-start) | copy-done | bytes 2097176
  3.5 0.0 copy-start.1
  3.5 0.9 %copy-done.1 = bf16[256,512]{1,0:T(8,128)(2,1)S(1)} copy-done((bf16[256,512]{1,0:T(8,128)(2,1)S(1)}, bf16[256,512]{1,0:T(8,128)(2,1)}, u32[]{:S(2)}) %copy-start.1) | copy-done | bytes 262168
  4.5 0.0 copy-start.2
  4.5 0.9 %copy-done.2 = bf16[128,512]{1,0:T(8,128)(2,1)S(1)} copy-done((bf16[128,512]{1,0:T(8,128)(2,1)S(1)}, bf16[128,512]{1,0:T(8,128)(2,1)}, u32[]{:S(2)}) %copy-start.2) | copy-done | bytes 131096
  5.4 0.0 copy-start.3
  5.4 0.9 %copy-done.3 = f32[3,512,16]{1,2,0:T(8,128)S(1)} copy-done((f32[3,512,16]{1,2,0:T(8,128)S(1)}, f32[3,512,16]{1,2,0:T(8,128)}, u32[]{:S(2)}) %copy-start.3) | copy-done | bytes 98328
  6.3 0.0 copy-start.4
  6.3 0.7 copy-done.4
  7.0 0.0 copy-start.5
  7.0 0.7 copy-done.5
  7.7 66.6 %key_projection.1 = (bf16[128,512]{1,0:T(8,128)(2,1)S(1)}, f32[3,16,512]{2,1,0:T(8,128)S(1)}, f32[3,16,32]{2,1,0:T(8,128)S(1)}, bf16[128,8192]{1,0:T(8,128)(2,1)S(1)}) custom-call(s32[1,1]{1,0:T(1,128)S(6)} %copy.16.off_ref, s32[1,1]{1,0:T(1,128)S(6)} %copy.17.cnt_ref, f32[1,128]{1,0:T(1,128)S(1)} %bitcast.5, f32[3,16,512]{2,1,0:T(8,128)S(1)} %bitcast.4, ...), custom_call_target="tpu_custom_call" | custom-call | tf_op jit(solution)/shard_map/key_projection/pallas_call | solution.py:411
  74.2 0.7 copy.18
  74.9 1.3 %copy.19 = bf16[128,8192]{1,0:T(8,128)(2,1)} copy(bf16[128,8192]{1,0:T(8,128)(2,1)S(1)} %get-tuple-element.17) | data formatting | bytes 4194304
  76.2 0.6 copy.20
  76.9 0.6 copy.21
Async XLA Ops:
  1.9 1.6 %copy-start = (bf16[128,8192]{1,0:T(8,128)(2,1)S(1)}, bf16[128,8192]{1,0:T(8,128)(2,1)}, u32[]{:S(2)}) copy-start(bf16[128,8192]{1,0:T(8,128)(2,1)} %tok_hbm.1) | copy-start | bytes 6291460
  3.5 0.9 %copy-start.1 = (bf16[256,512]{1,0:T(8,128)(2,1)S(1)}, bf16[256,512]{1,0:T(8,128)(2,1)}, u32[]{:S(2)}) copy-start(bf16[256,512]{1,0:T(8,128)(2,1)} %w_hbm.1) | copy-start | bytes 786436
  4.5 0.9 %copy-start.2 = (bf16[128,512]{1,0:T(8,128)(2,1)S(1)}, bf16[128,512]{1,0:T(8,128)(2,1)}, u32[]{:S(2)}) copy-start(bf16[128,512]{1,0:T(8,128)(2,1)} %cot_ref.1) | copy-start | bytes 393220
  5.4 0.9 %copy-start.3 = (f32[3,512,16]{1,2,0:T(8,128)S(1)}, f32[3,512,16]{1,2,0:T(8,128)}, u32[]{:S(2)}) copy-start(f32[3,512,16]{1,2,0:T(8,128)} %param.10) | copy-start | bytes 294916
  6.3 0.7 copy-start.4
  7.0 0.7 copy-start.5

commit v2 on v1

--- a/solution.py
+++ b/solution.py
@@ -35,10 +35,10 @@
 
 
 def kernel(
-    off_ref, cnt_ref, gain_ref, down_ref, up_ref, cot_ref, tok_hbm, w_hbm,
-    keys_ref, down_out, up_out, ig_hbm,
-    wf, tok, ig, acc, pg, meta, msg_out, msg_in, gmsg_out, gmsg_in, upf, ups,
-    loc_sem, ig_sem, zs, zr, ys, yr, xs, xr, ds_, dr, ms, mr, fs, fr, gs, gr,
+    off_ref, cnt_ref, gain_hbm, down_hbm, up_hbm, cot_hbm, tok_hbm, w_hbm,
+    keys_ref, down_out, up_out, ig,
+    gain_ref, down_ref, up_ref, cot_ref, wf, tok, acc, pg, meta, msg_out, msg_in, gmsg_out, gmsg_in, upf, ups,
+    loc_sem, zs, zr, ys, yr, xs, xr, ds_, dr, ms, mr, fs, fr, gs, gr,
 ):
     i, j = lax.axis_index("dp"), lax.axis_index("fsdp")
     yh, x = i // NX, i % NX
@@ -60,12 +60,21 @@
     def peer(r):
         return (i + r) % NDP
 
-    tok_copy = pltpu.make_async_copy(tok_hbm, tok, loc_sem.at[0])
-    tok_copy.start()
     pair_me = j // 2
-    own = pltpu.make_async_copy(w_hbm, wf.at[pair_me, pl.ds(pl.multiple_of(256 * c, 256), 256)], loc_sem.at[1])
-    own.start()
-
+    local = [
+        pltpu.make_async_copy(src, dst, loc_sem.at[n])
+        for n, (src, dst) in enumerate((
+            (w_hbm, wf.at[pair_me, pl.ds(pl.multiple_of(256 * c, 256), 256)]),
+            (down_hbm, down_ref),
+            (up_hbm, up_ref),
+            (tok_hbm, tok),
+            (gain_hbm, gain_ref),
+            (cot_hbm, cot_ref),
+        ))
+    ]
+    for copy in local:
+        copy.start()
+    own = local[0]
     off, cnt = off_ref[0, 0], cnt_ref[0, 0]
     rows8 = lax.broadcasted_iota(I32, (8, 128), 0)
     meta[i] = jnp.where(rows8 < 4, jnp.full((8, 128), off, I32), jnp.full((8, 128), cnt, I32))
@@ -170,6 +179,7 @@
 
     acc[...] = jnp.zeros_like(acc)
     ups[...] = jnp.zeros_like(ups)
+    local[2].wait()
     ups[:, :, 0:32] = up_ref[...]
     quarter = i % 4
 
@@ -198,6 +208,7 @@
         dst[:, 512:640] = hi
         dst[:, 640:768] = lo
 
+    local[1].wait()
     build(i, msg_in.at[i])
 
     @pl.loop(1, NDP)
@@ -210,7 +221,8 @@
         cols = pl.ds(pl.multiple_of(512 * q, 512), 512)
         acc[...] += dot(tok[:, cols], wf[q], PLAIN)
 
-    tok_copy.wait()
+    for copy in local[3:]:
+        copy.wait()
 
     wait_z(1)
     send_z(2)
@@ -348,17 +360,12 @@
 
     grads(i, gmsg_in.at[i])
 
-    def ig_copy(q):
-        cols = pl.ds(pl.multiple_of(512 * q, 512), 512)
-        return pltpu.make_async_copy(ig.at[:, cols], ig_hbm.at[:, cols], ig_sem.at[q])
-
     @pl.loop(0, NFS // 2)
     def _(q):
         cols = pl.ds(pl.multiple_of(512 * q, 512), 512)
         d = msg_in[q, :, 0:512]
         part = dot(lg2, jnp.concatenate([d, d], axis=0), PLAIN)
         ig[:, cols] = (part + dot(pre_low, wf[q], MINOR)).astype(BF)
-        ig_copy(q).start()
 
     def gather(p, sums):
         o = jnp.broadcast_to(meta[p][0:1, 0:1], (RANK, 512))
@@ -395,9 +402,37 @@
         remote(msg_out.at[p], msg_in.at[i], fs.at[r], fr.at[r], (p, j)).wait_send()
         remote(gmsg_out.at[p], gmsg_in.at[i], gs.at[r], gr.at[r], (p, j)).wait_send()
 
-    @pl.loop(0, NFS // 2)
-    def _(q):
-        ig_copy(q).wait()
+
+def put_kernel(*refs):
+    n = len(refs) // 2
+    sem = refs[-1]
+    copies = []
+    for src, dst in zip(refs[:n], refs[n : 2 * n], strict=True):
+        rows = src.shape[0]
+        parts = 8 if rows == 128 and src.shape[1] > 1024 else 1
+        for k in range(parts):
+            cut = pl.ds(k * (rows // parts), rows // parts)
+            copies.append(pltpu.make_async_copy(src.at[cut], dst.at[cut], sem.at[len(copies)]))
+    for copy in copies:
+        copy.start()
+    for copy in copies:
+        copy.wait()
+
+
+def put(*arrays):
+    hbm = pl.BlockSpec(memory_space=pltpu.MemorySpace.HBM)
+    return pl.pallas_call(
+        put_kernel,
+        out_shape=tuple(jax.ShapeDtypeStruct(a.shape, a.dtype) for a in arrays),
+        in_specs=[pl.BlockSpec(memory_space=pltpu.VMEM)] * len(arrays),
+        out_specs=(hbm,) * len(arrays),
+        scratch_shapes=[pltpu.SemaphoreType.DMA((16,))],
+        name="put",
+    )(*(pltpu.with_memory_space_constraint(a, pltpu.MemorySpace.VMEM) for a in arrays))
+
+
+def stay(a):
+    return pltpu.with_memory_space_constraint(a, pltpu.MemorySpace.HBM)
 
 
 def on_device(tokens, weight, down, up, gain, offset, count, cot):
@@ -405,22 +440,25 @@
     keys = cot.shape[1]
     vmem = pl.BlockSpec(memory_space=pltpu.VMEM)
     smem = pl.BlockSpec(memory_space=pltpu.SMEM)
-    anywhere = pl.BlockSpec(memory_space=pl.ANY)
+    hbm = pl.BlockSpec(memory_space=pltpu.MemorySpace.HBM)
     dma = pltpu.SemaphoreType.DMA
     down_t = jnp.transpose(down, (0, 2, 1))
     out = pl.pallas_call(
         kernel,
         out_shape=(
-            jax.ShapeDtypeStruct((n_rows, keys), BF),
-            jax.ShapeDtypeStruct(down_t.shape, F32),
-            jax.ShapeDtypeStruct(up.shape, F32),
-            jax.ShapeDtypeStruct((n_rows, width), BF),
+            pltpu.VMEM((n_rows, keys), BF),
+            pltpu.VMEM(down_t.shape, F32),
+            pltpu.VMEM(up.shape, F32),
+            pltpu.VMEM((n_rows, width), BF),
         ),
-        in_specs=[smem, smem, vmem, vmem, vmem, vmem, anywhere, anywhere],
-        out_specs=(vmem, vmem, vmem, anywhere),
+        in_specs=[smem] * 2 + [hbm] * 6,
+        out_specs=(vmem,) * 4,
         scratch_shapes=[
+            pltpu.VMEM((1, HD), F32),
+            pltpu.VMEM(down_t.shape, F32),
+            pltpu.VMEM(up.shape, F32),
+            pltpu.VMEM((n_rows, keys), BF),
             pltpu.VMEM((NFS // 2, 512, keys), BF),
-            pltpu.VMEM((n_rows, width), BF),
             pltpu.VMEM((n_rows, width), BF),
             pltpu.VMEM((n_rows, keys), F32),
             pltpu.VMEM((n_rows, keys), F32),
@@ -431,7 +469,7 @@
             pltpu.VMEM((NDP, RANK, 768), BF),
             pltpu.VMEM((RANK, keys), F32),
             pltpu.VMEM((SLOTS, RANK, 128), F32),
-            dma((2,)), dma((16,)),
+            dma((8,)),
             dma((8,)), dma((8,)),
             dma((16,)), dma((16,)),
             dma((32,)), dma((32,)),
@@ -444,8 +482,8 @@
             collective_id=0, has_side_effects=True, vmem_limit_bytes=40 * 1024 * 1024
         ),
         name="key_projection",
-    )(offset, count, gain.reshape(1, HD), down_t, up, cot, tokens, weight)
-    keys_out, down_grad, up_grad, input_grad = out
+    )(offset, count, *(stay(a) for a in (gain.reshape(1, HD), down_t, up, cot, tokens, weight)))
+    keys_out, down_grad, up_grad, input_grad = put(*out)
     return keys_out, input_grad, jnp.transpose(down_grad, (0, 2, 1)), up_grad
 
 

time: 77.8 us -> 69.9 us (0.90)
  local copies, waits for them, and re-layouts: 8.94 us -> 0 us
  Pallas kernels: 66.6 us -> 67.8 us
    unnamed x16 -> x0, local copies, waits for them, and re-layouts: 8.94 us -> none
    pallas_call x1 -> x2, Pallas kernels: 66.6 us -> 67.8 us  [the longest x1 66.2 us: on_device(): pl.pallas_call(kernel, out_shape=(pltpu.VMEM((n_rows, keys), BF), pltpu.V...]
where the time goes in v2:
time: 69.9 us; the launch traced here: 69.7 us
  Pallas kernels  67.8 us (97%)
  between operations  1.93 us (3%)
    pallas_call x1, Pallas kernels, on_device(): pl.pallas_call(kernel, out_shape=(pltpu.VMEM((n_rows, keys), BF), pltpu.V...  66.2 us
    pallas_call x1, Pallas kernels, put(): pl.pallas_call(put_kernel, out_shape=tuple((jax.ShapeDtypeStruct(a.shape,...  1.53 us

profile of v2, /device:TPU:1, one launch (start us, length us, event | category | flops | bytes accessed | tf_op | source)
XLA Modules:
  0.0 69.7 jit_solution(17262232571001213070)
XLA Ops:
  1.9 66.2 %key_projection.1 = (bf16[128,512]{1,0:T(8,128)(2,1)S(1)}, f32[3,16,512]{2,1,0:T(8,128)S(1)}, f32[3,16,32]{2,1,0:T(8,128)S(1)}, bf16[128,8192]{1,0:T(8,128)(2,1)S(1)}) custom-call(s32[1,1]{1,0:T(1,128)S(6)} %copy.12.off_ref, s32[1,1]{1,0:T(1,128)S(6)} %copy.13.cnt_ref, f32[1,128]{1,0:T(1,128)} %bitcast.4, f32[3,16,512]{2,1,0:T(8,128)} %bitcast.3, ...), custom_call_target="tpu_custom_call" | custom-call | tf_op jit(solution)/shard_map/key_projection/pallas_call | solution.py:446
  68.2 1.5 %put.1 = (bf16[128,512]{1,0:T(8,128)(2,1)}, f32[3,16,512]{2,1,0:T(8,128)}, f32[3,16,32]{2,1,0:T(8,128)}, bf16[128,8192]{1,0:T(8,128)(2,1)}) custom-call(bf16[128,512]{1,0:T(8,128)(2,1)S(1)} %get-tuple-element.12.refs_0_, f32[3,16,512]{2,1,0:T(8,128)S(1)} %get-tuple-element.13.refs_1_, f32[3,16,32]{2,1,0:T(8,128)S(1)} %get-tuple-element.14.refs_2_, ...), custom_call_target="tpu_custom_call" | custom-call | tf_op jit(solution)/shard_map/put/pallas_call | solution.py:424

commit v3 on v2

--- a/solution.py
+++ b/solution.py
@@ -16,13 +16,15 @@
 RANK = 16
 SLOTS = 3
 BF, F32, I32 = jnp.bfloat16, jnp.float32, jnp.int32
-HIGH = lax.Precision.HIGHEST
 MINOR = (((1,), (1,)), ((), ()))
 PLAIN = (((1,), (0,)), ((), ()))
 EXCL = 96
 FETCH = 256 - EXCL
 HALF = FETCH // 2
 XHALF = EXCL // 2
+
+
+ORDER = ((8, 12), (4, 8), (12, 16), (1, 4))
 
 
 def dot(a, b, dims, precision=None):
@@ -58,7 +60,18 @@
     x_dn = (dp_of(yh, (x + NX - 1) % NX), j)
 
     def peer(r):
-        return (i + r) % NDP
+        return dp_of((yh + r // NX) % NYH, (x + r % NX) % NX)
+
+    def source(r):
+        return dp_of((yh + NYH - r // NX) % NYH, (x + NX - r % NX) % NX)
+
+    def loops(who):
+        def run(body):
+            for first, last in ORDER:
+                pl.loop(first, last)(lambda r: body(r, who(r)))
+        return run
+
+    each, each_from = loops(peer), loops(source)
 
     pair_me = j // 2
     local = [
@@ -87,9 +100,9 @@
     for d in (z_up, z_dn, y_up, y_dn, sib):
         greet(d)
 
-    @pl.loop(1, NDP)
-    def _(r):
-        greet((peer(r), j))
+    @each
+    def _(r, p):
+        greet((p, j))
 
     pl.semaphore_wait(barrier, 5 + NDP - 1)
 
@@ -119,32 +132,29 @@
     def arrived(ref, ssem, rsem):
         remote(ref, ref, ssem, rsem, sib).wait_recv()
 
-    def z_piece(hop, dz):
-        if hop < 4:
-            return rows(dz, 0, f0, FETCH)
-        return rows(dz, 0, f0 if dz < 0 else f0 + HALF, HALF)
-
-    def send_z(hop):
-        send(z_piece(hop, -(hop - 1) if hop < 4 else -3), zs.at[hop - 1], zr.at[hop - 1], z_up)
-        send(z_piece(hop, hop - 1 if hop < 4 else 3), zs.at[3 + hop], zr.at[3 + hop], z_dn)
-
-    def wait_z(hop):
-        if hop < 4:
-            arrived(rows(-hop, 0, f0, FETCH), zs.at[hop - 1], zr.at[hop - 1])
-            arrived(rows(hop, 0, f0, FETCH), zs.at[3 + hop], zr.at[3 + hop])
-        else:
-            arrived(rows(4, 0, f0, HALF), zs.at[3], zr.at[3])
-            arrived(rows(4, 0, f0 + HALF, HALF), zs.at[7], zr.at[7])
-
-    def send_y(dz):
-        n = 2 * (dz + 3)
-        send(rows(dz, 0, f0, HALF), ys.at[n], yr.at[n], y_up)
-        send(rows(dz, 0, f0 + HALF, HALF), ys.at[n + 1], yr.at[n + 1], y_dn)
+    def chunk(dz, par, ch):
+        return rows(dz, par, f0 + HALF * ch, HALF)
+
+    def z_moves(hop, ch):
+        return [(8 * d + 2 * (hop - 1) + ch, sign, to) for d, (sign, to) in enumerate(((-1, z_up), (1, z_dn)))
+                if hop < 4 or d == ch]
+
+    def send_z(hop, ch):
+        for n, sign, to in z_moves(hop, ch):
+            send(chunk(sign * (hop - 1), 0, ch), zs.at[n], zr.at[n], to)
+
+    def wait_z(hop, ch):
+        for n, sign, _ in z_moves(hop, ch):
+            arrived(chunk(sign * hop if hop < 4 else 4, 0, ch), zs.at[n], zr.at[n])
+
+    def send_y(dz, ch):
+        n = 2 * (dz + 3) + ch
+        send(chunk(dz, 0, ch), ys.at[n], yr.at[n], y_dn if ch else y_up)
 
     def wait_y(dz):
-        n = 2 * (dz + 3)
-        arrived(rows(dz, 1, f0, HALF), ys.at[n], yr.at[n])
-        arrived(rows(dz, 1, f0 + HALF, HALF), ys.at[n + 1], yr.at[n + 1])
+        for ch in range(2):
+            n = 2 * (dz + 3) + ch
+            arrived(chunk(dz, 1, ch), ys.at[n], yr.at[n])
 
     def send_x(dz, par):
         n = 2 * spot[dz, par]
@@ -168,34 +178,48 @@
         arrived(ref, ds_.at[n], dr.at[n])
         return q
 
+    def both(step, k, *more):
+        step(-k, *more)
+        step(k, *more)
+
+    def wait_x_send_d(dz, par):
+        wait_x(dz, par)
+        send_d(dz, par)
+
+    def wait_y_send_x(dz):
+        wait_y(dz)
+        send_x(dz, 1)
+
+    def hop_on(hop):
+        for ch in range(2):
+            wait_z(hop, ch)
+            send_z(hop + 1, ch)
+            both(send_y, hop, ch)
+        both(send_x, hop, 0)
+
     own.wait()
-    send_z(1)
-    send_y(0)
+    for ch in range(2):
+        send_z(1, ch)
+        send_y(0, ch)
     send_d(0, 0)
 
-    @pl.loop(1, NDP)
-    def _(r):
-        remote(meta.at[i], meta.at[i], ms.at[r], mr.at[r], (peer(r), j)).start()
+    @each
+    def _(r, p):
+        remote(meta.at[i], meta.at[i], ms.at[r], mr.at[r], (p, j)).start()
 
     acc[...] = jnp.zeros_like(acc)
     ups[...] = jnp.zeros_like(ups)
     local[2].wait()
-    ups[:, :, 0:32] = up_ref[...]
-    quarter = i % 4
-
-    def placed(v):
-        out = v
-        for n in range(1, 4):
-            out = jnp.where(quarter == n, pltpu.roll(v, 32 * n, 1), out)
-        return out
-
-    for s in range(SLOTS):
-        ups[s] = placed(ups[s])
-
-    @pl.loop(1, NDP)
-    def _(r):
-        from_ = (i + NDP - r) % NDP
-        remote(meta.at[from_], meta.at[from_], ms.at[r], mr.at[r], sib).wait_recv()
+    u = up_ref[...]
+    high_part = u.astype(BF).astype(F32)
+    ups[:, :, 0:32] = high_part
+    ups[:, :, 32:64] = u - high_part
+
+    hop_on(1)
+
+    @each_from
+    def _(r, p):
+        remote(meta.at[p], meta.at[p], ms.at[r], mr.at[r], sib).wait_recv()
 
     def chosen(o, width, ref):
         o = jnp.broadcast_to(o[0:1, 0:1], (RANK, width))
@@ -204,122 +228,79 @@
     def build(p, dst):
         o = meta[p]
         dst[:, 0:512] = chosen(o, 512, down_ref).astype(BF)
-        hi, lo = split(chosen(o, 128, ups))
-        dst[:, 512:640] = hi
-        dst[:, 640:768] = lo
+        dst[:, 512:640] = chosen(o, 128, ups).astype(BF)
 
     local[1].wait()
-    build(i, msg_in.at[i])
-
-    @pl.loop(1, NDP)
-    def _(r):
-        p = peer(r)
+
+    @each
+    def _(r, p):
         build(p, msg_out.at[p])
         remote(msg_out.at[p], msg_in.at[i], fs.at[r], fr.at[r], (p, j)).start()
+
+    build(i, msg_in.at[i])
 
     def product(q):
         cols = pl.ds(pl.multiple_of(512 * q, 512), 512)
         acc[...] += dot(tok[:, cols], wf[q], PLAIN)
 
+    wait_y_send_x(0)
+    hop_on(2)
+    both(wait_y_send_x, 1)
+    both(wait_x_send_d, 1, 0)
     for copy in local[3:]:
         copy.wait()
-
-    wait_z(1)
-    send_z(2)
-    send_y(-1)
-    send_y(1)
-    send_x(-1, 0)
-    send_x(1, 0)
-    wait_y(0)
-    send_x(0, 1)
     product(wait_d(0, 0))
-    wait_z(2)
-    send_z(3)
-    send_y(-2)
-    send_y(2)
-    send_x(-2, 0)
-    send_x(2, 0)
-    wait_x(-1, 0)
-    send_d(-1, 0)
-    wait_x(1, 0)
-    send_d(1, 0)
-    wait_y(-1)
-    send_x(-1, 1)
-    wait_y(1)
-    send_x(1, 1)
-    wait_x(0, 1)
-    send_d(0, 1)
-    wait_z(3)
-    send_z(4)
-    send_y(-3)
-    send_y(3)
-    send_x(-3, 0)
-    send_x(3, 0)
-    wait_x(-2, 0)
-    send_d(-2, 0)
-    wait_x(2, 0)
-    send_d(2, 0)
-    wait_y(-2)
-    send_x(-2, 1)
-    wait_y(2)
-    send_x(2, 1)
-    wait_x(-1, 1)
-    send_d(-1, 1)
-    wait_x(1, 1)
-    send_d(1, 1)
-    product(wait_d(-1, 0))
-    product(wait_d(1, 0))
-    product(wait_d(0, 1))
-    wait_z(4)
-    send_y(4)
+    hop_on(3)
+    both(wait_y_send_x, 2)
+    wait_x_send_d(0, 1)
+    both(wait_x_send_d, 2, 0)
+    both(wait_x_send_d, 1, 1)
+    for place in ((-1, 0), (1, 0), (0, 1)):
+        product(wait_d(*place))
+    for ch in range(2):
+        wait_z(4, ch)
+        send_y(4, ch)
     send_x(4, 0)
-    wait_x(-3, 0)
-    send_d(-3, 0)
-    wait_x(3, 0)
-    send_d(3, 0)
-    wait_y(-3)
-    send_x(-3, 1)
-    wait_y(3)
-    send_x(3, 1)
-    wait_x(-2, 1)
-    send_d(-2, 1)
-    wait_x(2, 1)
-    send_d(2, 1)
-
-    @pl.loop(1, NDP)
-    def _(r):
-        from_ = (i + NDP - r) % NDP
-        remote(msg_in.at[from_], msg_in.at[from_], fs.at[r], fr.at[r], sib).wait_recv()
-
-    def low(p, total):
-        cols = pl.ds(pl.multiple_of(512 * p, 512), 512)
-        return total + dot(msg_in[p, :, 0:512], tok[:, cols], MINOR)
-
-    lr_t = lax.fori_loop(0, NDP, low, jnp.zeros((RANK, 128), F32))
+    both(wait_y_send_x, 3)
+    both(wait_x_send_d, 3, 0)
+    both(wait_x_send_d, 2, 1)
+    for place in ((-2, 0), (2, 0), (-1, 1), (1, 1)):
+        product(wait_d(*place))
+    wait_y_send_x(4)
+    wait_x_send_d(4, 0)
+    both(wait_x_send_d, 3, 1)
+
+    @each_from
+    def _(r, p):
+        remote(msg_in.at[p], msg_in.at[p], fs.at[r], fr.at[r], sib).wait_recv()
+
+    def low(n, total):
+        for k in range(4):
+            p = 4 * n + k
+            cols = pl.ds(pl.multiple_of(512 * p, 512), 512)
+            total += dot(msg_in[p, :, 0:512], tok[:, cols], MINOR)
+        return total
+
+    lr_t = lax.fori_loop(0, NDP // 4, low, jnp.zeros((RANK, 128), F32))
+    lane = lax.broadcasted_iota(I32, (RANK, 128), 1)
     for h in range(4):
         total = jnp.zeros((RANK, 128), F32)
         for q in range(4):
-            total += msg_in[4 * h + q, :, 512:640].astype(F32) + msg_in[4 * h + q, :, 640:768].astype(F32)
+            t = msg_in[4 * h + q, :, 512:640].astype(F32)
+            t = jnp.where(lane < 32, t + pltpu.roll(t, 96, 1), 0.0)
+            total += pltpu.roll(t, 32 * q, 1) if q else t
         upf[:, 128 * h : 128 * h + 128] = total
-    up = upf[...]
-
-    wait_y(4)
-    send_x(4, 1)
-    wait_x(4, 0)
-    send_d(4, 0)
-    wait_x(-3, 1)
-    send_d(-3, 1)
-    wait_x(3, 1)
-    send_d(3, 1)
-    for s in ((-2, 0), (2, 0), (-1, 1), (1, 1)):
-        product(wait_d(*s))
-    for s in ((-3, 0), (3, 0), (-2, 1), (2, 1)):
-        product(wait_d(*s))
-    extra = SCALE * dot(lr_t.T, up, PLAIN, HIGH)
-    wait_x(4, 1)
-    send_d(4, 1)
-    for s in ((4, 0), (-3, 1), (3, 1), (4, 1)):
-        product(wait_d(*s))
+    up_hi, up_lo = split(upf[...])
+    lr_hi, lr_lo = split(lr_t)
+    lr_hif, lr_lof = lr_hi.astype(F32), lr_lo.astype(F32)
+    lr3 = jnp.concatenate([lr_hif, lr_lof, lr_hif], axis=0).T.astype(BF)
+    extra = SCALE * dot(lr3, jnp.concatenate([up_hi, up_hi, up_lo], axis=0), PLAIN)
+    for place in ((-3, 0), (3, 0), (-2, 1), (2, 1)):
+        product(wait_d(*place))
+    acc[...] += extra
+    wait_x_send_d(4, 1)
+    for place in ((4, 0), (-3, 1), (3, 1), (4, 1)):
+        product(wait_d(*place))
 
     offs, cnts = meta[:, 0, :], meta[:, 4, :]
     total = jnp.sum(jnp.where(offs == off, cnts, 0), axis=0, keepdims=True).astype(F32)
@@ -328,37 +309,38 @@
     gain = gain_ref[...]
     for h in range(4):
         cols = slice(128 * h, 128 * h + 128)
-        projected = acc[:, cols] + extra[:, cols]
+        projected = acc[:, cols]
         inverse = lax.rsqrt(jnp.mean(projected * projected, axis=-1, keepdims=True) + EPS)
         normed = projected * inverse
         keys_ref[:, cols] = (normed * gain).astype(BF)
         scaled = cot_ref[:, cols].astype(F32) * row_scale * gain
         along = jnp.mean(scaled * normed, axis=-1, keepdims=True)
         pg[:, cols] = inverse * (scaled - normed * along)
-    pre = pg[...]
-    pre_low = pre.astype(BF)
-    lg_t = SCALE * dot(up, pre, MINOR, HIGH)
-    hi, lo = split(lg_t)
+    pre_low, pre_rest = split(pg[...])
+
+    def three(a_hi, a_lo, dims):
+        parts = dot(jnp.concatenate([a_hi, a_lo], axis=0), pre_low, dims)
+        return SCALE * (parts[0:RANK] + parts[RANK:] + dot(a_hi, pre_rest, dims))
+
+    hi, lo = split(three(up_hi, up_lo, MINOR))
     lg_t2 = jnp.concatenate([hi, lo], axis=0)
-    lg2 = jnp.concatenate([hi.astype(F32), lo.astype(F32)], axis=0).T.astype(BF)
-    upg = SCALE * dot(lr_t, pre, PLAIN, HIGH)
-    upf[...] = upg
+    upf[...] = three(lr_hi, lr_lo, PLAIN)
 
     def grads(p, dst):
         cols = pl.ds(pl.multiple_of(512 * p, 512), 512)
-        both = dot(lg_t2, tok[:, cols], PLAIN)
-        dst[:, 0:512] = (both[0:RANK] + both[RANK:]).astype(BF)
-        hi, lo = split(upf[:, pl.ds(pl.multiple_of(128 * (p // 4), 128), 128)])
-        dst[:, 512:640] = hi
-        dst[:, 640:768] = lo
-
-    @pl.loop(1, NDP)
-    def _(r):
-        p = peer(r)
+        parts = dot(lg_t2, tok[:, cols], PLAIN)
+        dst[:, 0:512] = (parts[0:RANK] + parts[RANK:]).astype(BF)
+        v = pltpu.roll(upf[:, pl.ds(pl.multiple_of(128 * (p // 4), 128), 128)], (128 - 32 * (p % 4)) % 128, 1)
+        rest = v - v.astype(BF).astype(F32)
+        dst[:, 512:640] = jnp.where(lane < 32, v, jnp.where(lane < 64, pltpu.roll(rest, 32, 1), 0.0)).astype(BF)
+
+    @each
+    def _(r, p):
         grads(p, gmsg_out.at[p])
         remote(gmsg_out.at[p], gmsg_in.at[i], gs.at[r], gr.at[r], (p, j)).start()
 
     grads(i, gmsg_in.at[i])
+    lg2 = jnp.concatenate([hi.astype(F32), lo.astype(F32)], axis=0).T.astype(BF)
 
     @pl.loop(0, NFS // 2)
     def _(q):
@@ -371,7 +353,7 @@
         o = jnp.broadcast_to(meta[p][0:1, 0:1], (RANK, 512))
         ou = o[:, 0:128]
         d = gmsg_in[p, :, 0:512].astype(F32)
-        u = gmsg_in[p, :, 512:640].astype(F32) + gmsg_in[p, :, 640:768].astype(F32)
+        u = gmsg_in[p, :, 512:640].astype(F32)
         return tuple(
             (sd + jnp.where(o == s, d, 0.0), su + jnp.where(ou == s, u, 0.0)) for s, (sd, su) in enumerate(sums)
         )
@@ -379,25 +361,21 @@
     zero = (jnp.zeros((RANK, 512), F32), jnp.zeros((RANK, 128), F32))
     sums = gather(i, (zero,) * SLOTS)
 
-    def later(r, sums):
-        from_ = (i + NDP - r) % NDP
-        remote(gmsg_in.at[from_], gmsg_in.at[from_], gs.at[r], gr.at[r], sib).wait_recv()
-        return gather(from_, sums)
-
-    sums = lax.fori_loop(1, NDP, later, sums)
+    def later(r, p, sums):
+        remote(gmsg_in.at[p], gmsg_in.at[p], gs.at[r], gr.at[r], sib).wait_recv()
+        return gather(p, sums)
+
+    for first, last in ORDER:
+        sums = lax.fori_loop(first, last, lambda r, t: later(r, source(r), t), sums)
     for s, (sd, su) in enumerate(sums):
         down_out[s] = sd
-        mine = su
-        for n in range(1, 4):
-            mine = jnp.where(quarter == n, pltpu.roll(su, 128 - 32 * n, 1), mine)
-        up_out[s] = mine[:, 0:32]
+        up_out[s] = (su + pltpu.roll(su, 96, 1))[:, 0:32]
 
     for copy in sends:
         copy.wait_send()
 
-    @pl.loop(1, NDP)
-    def _(r):
-        p = peer(r)
+    @each
+    def _(r, p):
         remote(meta.at[i], meta.at[i], ms.at[r], mr.at[r], (p, j)).wait_send()
         remote(msg_out.at[p], msg_in.at[i], fs.at[r], fr.at[r], (p, j)).wait_send()
         remote(gmsg_out.at[p], gmsg_in.at[i], gs.at[r], gr.at[r], (p, j)).wait_send()
@@ -463,14 +441,14 @@
             pltpu.VMEM((n_rows, keys), F32),
             pltpu.VMEM((n_rows, keys), F32),
             pltpu.VMEM((NDP, 8, 128), I32),
-            pltpu.VMEM((NDP, RANK, 768), BF),
-            pltpu.VMEM((NDP, RANK, 768), BF),
-            pltpu.VMEM((NDP, RANK, 768), BF),
-            pltpu.VMEM((NDP, RANK, 768), BF),
+            pltpu.VMEM((NDP, RANK, 640), BF),
+            pltpu.VMEM((NDP, RANK, 640), BF),
+            pltpu.VMEM((NDP, RANK, 640), BF),
+            pltpu.VMEM((NDP, RANK, 640), BF),
             pltpu.VMEM((RANK, keys), F32),
             pltpu.VMEM((SLOTS, RANK, 128), F32),
             dma((8,)),
-            dma((8,)), dma((8,)),
+            dma((16,)), dma((16,)),
             dma((16,)), dma((16,)),
             dma((32,)), dma((32,)),
             dma((16,)), dma((16,)),

time: 69.9 us -> 67.3 us (0.963)
  Pallas kernels: 67.8 us -> 65.3 us
    pallas_call x1, Pallas kernels: 66.2 us -> 63.7 us  [on_device(): pl.pallas_call(kernel, out_shape=(pltpu.VMEM((n_rows, keys), BF), pltpu.V...]
where the time goes in v3:
time: 67.3 us; the launch traced here: 67.2 us
  Pallas kernels  65.3 us (97%)
  between operations  1.93 us (3%)
    pallas_call x1, Pallas kernels, on_device(): pl.pallas_call(kernel, out_shape=(pltpu.VMEM((n_rows, keys), BF), pltpu.V...  63.7 us
    pallas_call x1, Pallas kernels, put(): pl.pallas_call(put_kernel, out_shape=tuple((jax.ShapeDtypeStruct(a.shape,...  1.53 us

profile of v3, /device:TPU:1, one launch (start us, length us, event | category | flops | bytes accessed | tf_op | source)
XLA Modules:
  0.0 67.2 jit_solution(14658012553640507655)
XLA Ops:
  1.9 63.7 %key_projection.1 = (bf16[128,512]{1,0:T(8,128)(2,1)S(1)}, f32[3,16,512]{2,1,0:T(8,128)S(1)}, f32[3,16,32]{2,1,0:T(8,128)S(1)}, bf16[128,8192]{1,0:T(8,128)(2,1)S(1)}) custom-call(s32[1,1]{1,0:T(1,128)S(6)} %copy.12.off_ref, s32[1,1]{1,0:T(1,128)S(6)} %copy.13.cnt_ref, f32[1,128]{1,0:T(1,128)} %bitcast.4, f32[3,16,512]{2,1,0:T(8,128)} %bitcast.3, ...), custom_call_target="tpu_custom_call" | custom-call | tf_op jit(solution)/shard_map/key_projection/pallas_call | solution.py:424
  65.7 1.5 %put.1 = (bf16[128,512]{1,0:T(8,128)(2,1)}, f32[3,16,512]{2,1,0:T(8,128)}, f32[3,16,32]{2,1,0:T(8,128)}, bf16[128,8192]{1,0:T(8,128)(2,1)}) custom-call(bf16[128,512]{1,0:T(8,128)(2,1)S(1)} %get-tuple-element.12.refs_0_, f32[3,16,512]{2,1,0:T(8,128)S(1)} %get-tuple-element.13.refs_1_, f32[3,16,32]{2,1,0:T(8,128)S(1)} %get-tuple-element.14.refs_2_, ...), custom_call_target="tpu_custom_call" | custom-call | tf_op jit(solution)/shard_map/put/pallas_call | solution.py:402

commit v4 on v3

--- a/solution.py
+++ b/solution.py
@@ -65,13 +65,13 @@
     def source(r):
         return dp_of((yh + NYH - r // NX) % NYH, (x + NX - r % NX) % NX)
 
-    def loops(who):
+    def loops(who, unroll):
         def run(body):
             for first, last in ORDER:
-                pl.loop(first, last)(lambda r: body(r, who(r)))
+                pl.loop(first, last, unroll=last - first if unroll else 1)(lambda r: body(r, who(r)))
         return run
 
-    each, each_from = loops(peer), loops(source)
+    each, each_from, each_unrolled = loops(peer, False), loops(source, False), loops(peer, True)
 
     pair_me = j // 2
     local = [
@@ -194,8 +194,11 @@
         for ch in range(2):
             wait_z(hop, ch)
             send_z(hop + 1, ch)
-            both(send_y, hop, ch)
+            if hop > 1:
+                both(send_y, hop, ch)
         both(send_x, hop, 0)
+
+    beside = ((7, -1, z_up), (14, 1, z_dn))
 
     own.wait()
     for ch in range(2):
@@ -216,6 +219,9 @@
     ups[:, :, 32:64] = u - high_part
 
     hop_on(1)
+    wait_y_send_x(0)
+    for n, _, to in beside:
+        send(rows(0, 1, f0, FETCH), zs.at[n], zr.at[n], to)
 
     @each_from
     def _(r, p):
@@ -232,7 +238,7 @@
 
     local[1].wait()
 
-    @each
+    @each_unrolled
     def _(r, p):
         build(p, msg_out.at[p])
         remote(msg_out.at[p], msg_in.at[i], fs.at[r], fr.at[r], (p, j)).start()
@@ -243,18 +249,18 @@
         cols = pl.ds(pl.multiple_of(512 * q, 512), 512)
         acc[...] += dot(tok[:, cols], wf[q], PLAIN)
 
-    wait_y_send_x(0)
     hop_on(2)
-    both(wait_y_send_x, 1)
     both(wait_x_send_d, 1, 0)
     for copy in local[3:]:
         copy.wait()
     product(wait_d(0, 0))
     hop_on(3)
+    for n, sign, _ in beside:
+        arrived(rows(sign, 1, f0, FETCH), zs.at[n], zr.at[n])
+        send_x(sign, 1)
     both(wait_y_send_x, 2)
     wait_x_send_d(0, 1)
     both(wait_x_send_d, 2, 0)
-    both(wait_x_send_d, 1, 1)
     for place in ((-1, 0), (1, 0), (0, 1)):
         product(wait_d(*place))
     for ch in range(2):
@@ -262,6 +268,7 @@
         send_y(4, ch)
     send_x(4, 0)
     both(wait_y_send_x, 3)
+    both(wait_x_send_d, 1, 1)
     both(wait_x_send_d, 3, 0)
     both(wait_x_send_d, 2, 1)
     for place in ((-2, 0), (2, 0), (-1, 1), (1, 1)):
@@ -334,7 +341,7 @@
         rest = v - v.astype(BF).astype(F32)
         dst[:, 512:640] = jnp.where(lane < 32, v, jnp.where(lane < 64, pltpu.roll(rest, 32, 1), 0.0)).astype(BF)
 
-    @each
+    @each_unrolled
     def _(r, p):
         grads(p, gmsg_out.at[p])
         remote(gmsg_out.at[p], gmsg_in.at[i], gs.at[r], gr.at[r], (p, j)).start()
@@ -342,7 +349,7 @@
     grads(i, gmsg_in.at[i])
     lg2 = jnp.concatenate([hi.astype(F32), lo.astype(F32)], axis=0).T.astype(BF)
 
-    @pl.loop(0, NFS // 2)
+    @pl.loop(0, NFS // 2, unroll=4)
     def _(q):
         cols = pl.ds(pl.multiple_of(512 * q, 512), 512)
         d = msg_in[q, :, 0:512]
@@ -366,7 +373,7 @@
         return gather(p, sums)
 
     for first, last in ORDER:
-        sums = lax.fori_loop(first, last, lambda r, t: later(r, source(r), t), sums)
+        sums = lax.fori_loop(first, last, lambda r, t: later(r, source(r), t), sums, unroll=True)
     for s, (sd, su) in enumerate(sums):
         down_out[s] = sd
         up_out[s] = (su + pltpu.roll(su, 96, 1))[:, 0:32]

time: 67.3 us -> 64 us (0.951)
  Pallas kernels: 65.3 us -> 61.9 us
    pallas_call x1, Pallas kernels: 63.7 us -> 60.4 us  [on_device(): pl.pallas_call(kernel, out_shape=(pltpu.VMEM((n_rows, keys), BF), pltpu.V...]
where the time goes in v4:
time: 64 us; the launch traced here: 63.9 us
  Pallas kernels  61.9 us (97%)
  between operations  1.93 us (3%)
    pallas_call x1, Pallas kernels, on_device(): pl.pallas_call(kernel, out_shape=(pltpu.VMEM((n_rows, keys), BF), pltpu.V...  60.4 us
    pallas_call x1, Pallas kernels, put(): pl.pallas_call(put_kernel, out_shape=tuple((jax.ShapeDtypeStruct(a.shape,...  1.53 us

profile of v4, /device:TPU:1, one launch (start us, length us, event | category | flops | bytes accessed | tf_op | source)
XLA Modules:
  0.0 63.9 jit_solution(13899637230629317983)
XLA Ops:
  1.9 60.4 %key_projection.1 = (bf16[128,512]{1,0:T(8,128)(2,1)S(1)}, f32[3,16,512]{2,1,0:T(8,128)S(1)}, f32[3,16,32]{2,1,0:T(8,128)S(1)}, bf16[128,8192]{1,0:T(8,128)(2,1)S(1)}) custom-call(s32[1,1]{1,0:T(1,128)S(6)} %copy.12.off_ref, s32[1,1]{1,0:T(1,128)S(6)} %copy.13.cnt_ref, f32[1,128]{1,0:T(1,128)} %bitcast.4, f32[3,16,512]{2,1,0:T(8,128)} %bitcast.3, ...), custom_call_target="tpu_custom_call" | custom-call | tf_op jit(solution)/shard_map/key_projection/pallas_call | solution.py:431
  62.3 1.5 %put.1 = (bf16[128,512]{1,0:T(8,128)(2,1)}, f32[3,16,512]{2,1,0:T(8,128)}, f32[3,16,32]{2,1,0:T(8,128)}, bf16[128,8192]{1,0:T(8,128)(2,1)}) custom-call(bf16[128,512]{1,0:T(8,128)(2,1)S(1)} %get-tuple-element.12.refs_0_, f32[3,16,512]{2,1,0:T(8,128)S(1)} %get-tuple-element.13.refs_1_, f32[3,16,32]{2,1,0:T(8,128)S(1)} %get-tuple-element.14.refs_2_, ...), custom_call_target="tpu_custom_call" | custom-call | tf_op jit(solution)/shard_map/put/pallas_call | solution.py:409

commit v5 on v4

--- a/solution.py
+++ b/solution.py
@@ -245,15 +245,18 @@
 
     build(i, msg_in.at[i])
 
-    def product(q):
-        cols = pl.ds(pl.multiple_of(512 * q, 512), 512)
-        acc[...] += dot(tok[:, cols], wf[q], PLAIN)
+    def products(*places):
+        total = acc[...]
+        for place in places:
+            q = wait_d(*place)
+            total += dot(tok[:, pl.ds(pl.multiple_of(512 * q, 512), 512)], wf[q], PLAIN)
+        acc[...] = total
 
     hop_on(2)
     both(wait_x_send_d, 1, 0)
     for copy in local[3:]:
         copy.wait()
-    product(wait_d(0, 0))
+    products((0, 0))
     hop_on(3)
     for n, sign, _ in beside:
         arrived(rows(sign, 1, f0, FETCH), zs.at[n], zr.at[n])
@@ -261,8 +264,22 @@
     both(wait_y_send_x, 2)
     wait_x_send_d(0, 1)
     both(wait_x_send_d, 2, 0)
-    for place in ((-1, 0), (1, 0), (0, 1)):
-        product(wait_d(*place))
+    products((-1, 0), (1, 0), (0, 1))
+    def low_of(p):
+        cols = pl.ds(pl.multiple_of(512 * p, 512), 512)
+        return dot(msg_in[p, :, 0:512], tok[:, cols], MINOR)
+
+    def low(group, total):
+        @pl.loop(*group)
+        def _(r):
+            p = source(r)
+            remote(msg_in.at[p], msg_in.at[p], fs.at[r], fr.at[r], sib).wait_recv()
+
+        for r in range(*group):
+            total += low_of(source(r))
+        return total
+
+    lr_t = low_of(i)
     for ch in range(2):
         wait_z(4, ch)
         send_y(4, ch)
@@ -271,24 +288,22 @@
     both(wait_x_send_d, 1, 1)
     both(wait_x_send_d, 3, 0)
     both(wait_x_send_d, 2, 1)
-    for place in ((-2, 0), (2, 0), (-1, 1), (1, 1)):
-        product(wait_d(*place))
+    products((-2, 0), (2, 0), (-1, 1), (1, 1))
     wait_y_send_x(4)
     wait_x_send_d(4, 0)
     both(wait_x_send_d, 3, 1)
 
-    @each_from
-    def _(r, p):
-        remote(msg_in.at[p], msg_in.at[p], fs.at[r], fr.at[r], sib).wait_recv()
-
-    def low(n, total):
-        for k in range(4):
-            p = 4 * n + k
-            cols = pl.ds(pl.multiple_of(512 * p, 512), 512)
-            total += dot(msg_in[p, :, 0:512], tok[:, cols], MINOR)
-        return total
-
-    lr_t = lax.fori_loop(0, NDP // 4, low, jnp.zeros((RANK, 128), F32))
+    offs, cnts = meta[:, 0, :], meta[:, 4, :]
+    total = jnp.sum(jnp.where(offs == off, cnts, 0), axis=0, keepdims=True).astype(F32)
+    live = lax.broadcasted_iota(I32, (128, 128), 0) < cnt
+    row_scale = jnp.where(live, jnp.broadcast_to(128.0 / total, (128, 128)), 0.0)
+    gain = gain_ref[...]
+    for h in range(4):
+        cols = slice(128 * h, 128 * h + 128)
+        pg[:, cols] = cot_ref[:, cols].astype(F32) * row_scale * gain
+
+    for group in ((1, 4), (12, 16), (4, 8), (8, 12)):
+        lr_t = low(group, lr_t)
     lane = lax.broadcasted_iota(I32, (RANK, 128), 1)
     for h in range(4):
         total = jnp.zeros((RANK, 128), F32)
@@ -302,25 +317,18 @@
     lr_hif, lr_lof = lr_hi.astype(F32), lr_lo.astype(F32)
     lr3 = jnp.concatenate([lr_hif, lr_lof, lr_hif], axis=0).T.astype(BF)
     extra = SCALE * dot(lr3, jnp.concatenate([up_hi, up_hi, up_lo], axis=0), PLAIN)
-    for place in ((-3, 0), (3, 0), (-2, 1), (2, 1)):
-        product(wait_d(*place))
+    products((-3, 0), (3, 0), (-2, 1), (2, 1))
     acc[...] += extra
     wait_x_send_d(4, 1)
-    for place in ((4, 0), (-3, 1), (3, 1), (4, 1)):
-        product(wait_d(*place))
-
-    offs, cnts = meta[:, 0, :], meta[:, 4, :]
-    total = jnp.sum(jnp.where(offs == off, cnts, 0), axis=0, keepdims=True).astype(F32)
-    live = lax.broadcasted_iota(I32, (128, 128), 0) < cnt
-    row_scale = jnp.where(live, jnp.broadcast_to(128.0 / total, (128, 128)), 0.0)
-    gain = gain_ref[...]
+    products((4, 0), (-3, 1), (3, 1), (4, 1))
+
     for h in range(4):
         cols = slice(128 * h, 128 * h + 128)
         projected = acc[:, cols]
         inverse = lax.rsqrt(jnp.mean(projected * projected, axis=-1, keepdims=True) + EPS)
         normed = projected * inverse
         keys_ref[:, cols] = (normed * gain).astype(BF)
-        scaled = cot_ref[:, cols].astype(F32) * row_scale * gain
+        scaled = pg[:, cols]
         along = jnp.mean(scaled * normed, axis=-1, keepdims=True)
         pg[:, cols] = inverse * (scaled - normed * along)
     pre_low, pre_rest = split(pg[...])

time: 64 us -> 64.2 us (level)
  no operation moved by 1% of the time
where the time goes in v5:
time: 64.2 us; the launch traced here: 64 us
  Pallas kernels  62.1 us (97%)
  between operations  1.93 us (3%)
    pallas_call x1, Pallas kernels, on_device(): pl.pallas_call(kernel, out_shape=(pltpu.VMEM((n_rows, keys), BF), pltpu.V...  60.6 us
    pallas_call x1, Pallas kernels, put(): pl.pallas_call(put_kernel, out_shape=tuple((jax.ShapeDtypeStruct(a.shape,...  1.53 us

profile of v5, /device:TPU:1, one launch (start us, length us, event | category | flops | bytes accessed | tf_op | source)
XLA Modules:
  0.0 64.0 jit_solution(12813880278070789006)
XLA Ops:
  1.9 60.6 %key_projection.1 = (bf16[128,512]{1,0:T(8,128)(2,1)S(1)}, f32[3,16,512]{2,1,0:T(8,128)S(1)}, f32[3,16,32]{2,1,0:T(8,128)S(1)}, bf16[128,8192]{1,0:T(8,128)(2,1)S(1)}) custom-call(s32[1,1]{1,0:T(1,128)S(6)} %copy.12.off_ref, s32[1,1]{1,0:T(1,128)S(6)} %copy.13.cnt_ref, f32[1,128]{1,0:T(1,128)} %bitcast.4, f32[3,16,512]{2,1,0:T(8,128)} %bitcast.3, ...), custom_call_target="tpu_custom_call" | custom-call | tf_op jit(solution)/shard_map/key_projection/pallas_call | solution.py:439
  62.5 1.5 %put.1 = (bf16[128,512]{1,0:T(8,128)(2,1)}, f32[3,16,512]{2,1,0:T(8,128)}, f32[3,16,32]{2,1,0:T(8,128)}, bf16[128,8192]{1,0:T(8,128)(2,1)}) custom-call(bf16[128,512]{1,0:T(8,128)(2,1)S(1)} %get-tuple-element.12.refs_0_, f32[3,16,512]{2,1,0:T(8,128)S(1)} %get-tuple-element.13.refs_1_, f32[3,16,32]{2,1,0:T(8,128)S(1)} %get-tuple-element.14.refs_2_, ...), custom_call_target="tpu_custom_call" | custom-call | tf_op jit(solution)/shard_map/put/pallas_call | solution.py:417
